TPU v7x, 32 devices: a whole 2x2x4 slice. The times are simulated.
32 devices in a mesh: ex: 4 (over y, x), ey: 2 (over core), tp: 4 (over z).
Axes of the slice: x: 2, y: 2, z: 4, core: 2. Of those that a mesh axis runs over, the one named last changes fastest.
Arguments:
- tokens: bfloat16 [256, 7168], P(('ex', 'ey'), 'tp'), may hold values from -6 to 6
- cotangent: bfloat16 [256, 7168], P(('ex', 'ey'), 'tp'), may hold values from -0.59765625 to 0.59765625
- gates: bfloat16 [256, 8], P(('ex', 'ey')), may hold values from 0.049804688 to 1
- expert_ids: int32 [256, 8], P(('ex', 'ey')), may hold values from 0 to 31, all different within a row; in each aligned block of 32 rows (0 to 31, 32 to 63, ...) at most 10 rows name the same one
- saved_gate: bfloat16 [1024, 32, 80], P(None, ('ex', 'ey')), may hold values from -6 to 6
- saved_up: bfloat16 [1024, 32, 80], P(None, ('ex', 'ey')), may hold values from -6 to 6
- w_gate: bfloat16 [32, 7168, 1024], P(('ex', 'ey'), 'tp'), may hold values from -0.1875 to 0.1875
- w_up: bfloat16 [32, 7168, 1024], P(('ex', 'ey'), 'tp'), may hold values from -0.1875 to 0.1875
- w_down: bfloat16 [32, 1024, 7168], P(('ex', 'ey'), None, 'tp'), may hold values from -0.25 to 0.25
Outputs:
- grad_tokens: bfloat16 [256, 7168], P(('ex', 'ey'), 'tp')
- grad_gates: bfloat16 [256, 8], P(('ex', 'ey'))
- grad_w_gate: bfloat16 [32, 7168, 1024], P(('ex', 'ey'), 'tp')
- grad_w_up: bfloat16 [32, 7168, 1024], P(('ex', 'ey'), 'tp')
- grad_w_down: bfloat16 [32, 1024, 7168], P(('ex', 'ey'), None, 'tp')
Inputs may be any that keep to these rules, and one draw needn't show every extreme that they name: `expert_ids`: each row names 8 different experts. The rows of one token group name any one expert at most 10 times, a bound that some block reaches.
All inputs are finite; a program needn't handle non-finite values.
Results may differ from a plain program's by a relative error of at most 0.025.
Values may be sent and summed in bfloat16 or wider, within the bound.
A program may use at most 128 MiB of HBM per device.

v0:
```python
import jax
import jax.numpy as jnp
from jax import lax
from jax.sharding import PartitionSpec as P

EXPERTS = 32
TOP = 8
CAP = 10


def slot_codes(expert_ids, capacity, expert_count):
    tok_rows, top_count = expert_ids.shape
    flat = expert_ids.reshape(-1)
    onehot = (flat[:, None] == jnp.arange(expert_count, dtype=jnp.int32)[None, :]).astype(jnp.int32)
    before = jnp.cumsum(onehot, axis=0) - onehot
    position = jnp.sum(before * onehot, axis=1)
    return (flat * capacity + position).reshape(tok_rows, top_count)


def pre_grads(dh_rows, gate_rows, up_rows):
    dh_wide = dh_rows.astype(jnp.float32)
    act_gate = gate_rows.astype(jnp.float32)
    act_up = up_rows.astype(jnp.float32)
    sigm = jax.nn.sigmoid(act_gate)
    d_gate_pre = (dh_wide * act_up * sigm * (1.0 + act_gate * (1.0 - sigm))).astype(jnp.bfloat16)
    d_up_pre = (dh_wide * act_gate * sigm).astype(jnp.bfloat16)
    return (d_gate_pre, d_up_pre)


def on_device(tokens, cotangent, gates, expert_ids, saved_gate, saved_up, w_gate, w_up, w_down):
    expert_count = EXPERTS
    capacity = CAP
    top_count = TOP
    local_width = tokens.shape[1]
    codes = slot_codes(expert_ids, capacity, expert_count)
    slot_rows = jnp.arange(expert_count * capacity, dtype=jnp.int32)
    tables = [
        (codes[:, k][None, :] == slot_rows[:, None]).astype(jnp.bfloat16) for k in range(top_count)
    ]
    chosen = tables[0]
    send_gate = jnp.dot(tables[0], gates[:, 0:1], preferred_element_type=jnp.float32)
    for k in range(1, top_count):
        chosen = chosen + tables[k]
        send_gate = send_gate + jnp.dot(
            tables[k], gates[:, k : k + 1], preferred_element_type=jnp.float32
        )
    send_x = jnp.dot(chosen, tokens, preferred_element_type=jnp.float32).astype(jnp.bfloat16)
    send_dy = jnp.dot(chosen, cotangent, preferred_element_type=jnp.float32).astype(jnp.bfloat16)
    send_x = send_x.reshape(expert_count, capacity, local_width)
    send_dy = send_dy.reshape(expert_count, capacity, local_width)
    send_gate = send_gate.astype(jnp.bfloat16).reshape(expert_count, capacity, 1)
    recv_x, recv_dy, recv_gate = (
        lax.all_to_all(send_x, ("ex", "ey"), split_axis=0, concat_axis=1, tiled=True),
        lax.all_to_all(send_dy, ("ex", "ey"), split_axis=0, concat_axis=1, tiled=True),
        lax.all_to_all(send_gate, ("ex", "ey"), split_axis=0, concat_axis=1, tiled=True),
    )
    scaled = (recv_gate.astype(jnp.float32) * recv_dy.astype(jnp.float32)).astype(jnp.bfloat16)
    gate_act = saved_gate.astype(jnp.float32)
    hidden = (gate_act * jax.nn.sigmoid(gate_act) * saved_up.astype(jnp.float32)).astype(
        jnp.bfloat16
    )
    out_rows = jnp.einsum("fes,efd->esd", hidden, w_down, preferred_element_type=jnp.float32)
    score_part = jnp.sum(recv_dy.astype(jnp.float32) * out_rows, axis=2).astype(jnp.bfloat16)
    dh_local = lax.psum_scatter(
        jnp.einsum("efd,esd->fes", w_down, scaled, preferred_element_type=jnp.float32).astype(
            jnp.bfloat16
        ),
        "tp",
        scatter_dimension=0,
        tiled=True,
    )
    dh_full, score_parts = (
        lax.all_gather(dh_local, "tp", axis=0, tiled=True),
        lax.all_gather(score_part[None], "tp", axis=0, tiled=True),
    )
    d_gate_pre, d_up_pre = pre_grads(dh_full, saved_gate, saved_up)
    score = jnp.sum(score_parts.astype(jnp.float32), axis=0).astype(jnp.bfloat16)
    dx_rows = jnp.einsum("fes,edf->esd", d_gate_pre, w_gate, preferred_element_type=jnp.float32)
    dx_rows = dx_rows + jnp.einsum(
        "fes,edf->esd", d_up_pre, w_up, preferred_element_type=jnp.float32
    )
    dx_rows = dx_rows.astype(jnp.bfloat16)
    grad_w_gate = jnp.einsum(
        "esd,fes->edf", recv_x, d_gate_pre, preferred_element_type=jnp.float32
    ).astype(jnp.bfloat16)
    grad_w_up = jnp.einsum(
        "esd,fes->edf", recv_x, d_up_pre, preferred_element_type=jnp.float32
    ).astype(jnp.bfloat16)
    grad_w_down = jnp.einsum(
        "fes,esd->efd", hidden, scaled, preferred_element_type=jnp.float32
    ).astype(jnp.bfloat16)
    score_col = score[:, :, None]
    back_dx, back_score = (
        lax.all_to_all(dx_rows, ("ex", "ey"), split_axis=1, concat_axis=0, tiled=True),
        lax.all_to_all(score_col, ("ex", "ey"), split_axis=1, concat_axis=0, tiled=True),
    )
    flat_dx = back_dx.reshape(expert_count * capacity, local_width)
    contract = (((0,), (0,)), ((), ()))
    grad_tokens = lax.dot_general(
        chosen, flat_dx, contract, preferred_element_type=jnp.float32
    ).astype(jnp.bfloat16)
    flat_score = back_score.reshape(expert_count * capacity, 1)
    columns = [
        lax.dot_general(tables[k], flat_score, contract, preferred_element_type=jnp.float32)
        for k in range(top_count)
    ]
    grad_gates = jnp.concatenate(columns, axis=1).astype(jnp.bfloat16)
    return (grad_tokens, grad_gates, grad_w_gate, grad_w_up, grad_w_down)


def solution(mesh):
    in_specs = (
        P(("ex", "ey"), "tp"),
        P(("ex", "ey"), "tp"),
        P(("ex", "ey"), None),
        P(("ex", "ey"), None),
        P(None, ("ex", "ey"), None),
        P(None, ("ex", "ey"), None),
        P(("ex", "ey"), "tp", None),
        P(("ex", "ey"), "tp", None),
        P(("ex", "ey"), None, "tp"),
    )
    out_specs = (
        P(("ex", "ey"), "tp"),
        P(("ex", "ey"), None),
        P(("ex", "ey"), "tp", None),
        P(("ex", "ey"), "tp", None),
        P(("ex", "ey"), None, "tp"),
    )
    return jax.shard_map(
        on_device, mesh=mesh, in_specs=in_specs, out_specs=out_specs, check_vma=False
    )
```

profile of v0, /device:TPU:0, one launch (start us, length us, event | category | flops | bytes accessed | tf_op | source)
XLA Modules:
  0.0 181.6 jit_solution(12350616389639696154)
XLA Ops:
  7.2 0.0 copy-start
  7.2 0.8 copy.64
  8.0 0.1 eq.145
  8.1 0.1 eq.149
  8.2 0.6 reduce-window.6
  8.8 0.2 slice_reduce_fusion
  9.0 0.1 fusion.66
  9.1 0.1 reduce_sum.33
  9.2 0.3 slice_reduce_fusion.7
  9.5 0.9 convolution_reduce_fusion
  10.4 0.9 convolution_reduce_fusion.1
  11.2 0.9 convolution_reduce_fusion.2
  12.1 0.9 convolution_reduce_fusion.3
  12.9 0.9 convolution_reduce_fusion.4
  13.8 0.9 convolution_reduce_fusion.5
  14.6 0.9 convolution_reduce_fusion.7
  15.5 0.9 convolution_reduce_fusion.6
  16.4 0.7 reshape.205
  17.1 5.2 %all-to-all-start = ((bf16[32,10,1]{1,2,0:T(2,128)(2,1)}), bf16[32,10,1]{1,2,0:T(2,128)(2,1)S(1)}, u32[]{:S(2)}, u32[]{:S(2)}) async-start(bf16[32,10,1]{1,2,0:T(2,128)(2,1)} %reshape.205), calls=%async_computation | async-start | bytes 32768 | tf_op jit(solution)/shard_map/all_to_all | solution.py:55
  22.3 0.5 convolution_convert_fusion.4
  22.8 1.4 reshape.161
  24.2 2.8 %all-to-all-done = bf16[32,10,1]{1,2,0:T(2,128)(2,1)S(1)} async-done(((bf16[32,10,1]{1,2,0:T(2,128)(2,1)}), bf16[32,10,1]{1,2,0:T(2,128)(2,1)S(1)}, u32[]{:S(2)}, u32[]{:S(2)}) %all-to-all-start) | async-done | bytes 672 | tf_op jit(solution)/shard_map/all_to_all | solution.py:55
  27.0 3.6 %all-to-all-start.1 = ((bf16[32,10,1792]{2,1,0:T(8,128)(2,1)}), bf16[32,10,1792]{2,1,0:T(8,128)(2,1)S(1)}, u32[]{:S(2)}, u32[]{:S(2)}) async-start(bf16[32,10,1792]{2,1,0:T(8,128)(2,1)} %reshape.161), calls=%async_computation.1 | async-start | bytes 3670016 | tf_op jit(solution)/shard_map/all_to_all | solution.py:54
  30.7 0.5 convolution_convert_fusion.3
  31.2 1.4 reshape.164
  32.6 0.1 reshape.165
  32.7 0.1 copy.71
  32.8 21.6 %all-to-all-done.1 = bf16[32,10,1792]{2,1,0:T(8,128)(2,1)S(1)} async-done(((bf16[32,10,1792]{2,1,0:T(8,128)(2,1)}), bf16[32,10,1792]{2,1,0:T(8,128)(2,1)S(1)}, u32[]{:S(2)}, u32[]{:S(2)}) %all-to-all-start.1) | async-done | bytes 1146912 | tf_op jit(solution)/shard_map/all_to_all | solution.py:54
  54.4 4.3 %all-to-all-start.4 = ((bf16[32,10,1792]{2,1,0:T(8,128)(2,1)}), bf16[32,10,1792]{2,1,0:T(8,128)(2,1)}, u32[]{:S(2)}, u32[]{:S(2)}) async-start(bf16[32,10,1792]{2,1,0:T(8,128)(2,1)} %reshape.164), calls=%async_computation.5 | async-start | bytes 3670016 | tf_op jit(solution)/shard_map/all_to_all | solution.py:53
  58.7 0.0 reduce-scatter.2.cloned.1.call-start
  58.7 0.6 copy.72
  59.4 1.4 copy-done.3
  60.7 0.6 multiply_convert_fusion
  61.3 10.6 %fusion.12 = bf16[1024,4,80]{0,2,1:T(8,128)(2,1)} fusion(bf16[4,1024,1792]{2,1,0:T(8,128)(2,1)} %param.17, bf16[4,80,1792]{2,0,1:T(4,128)(2,1)S(1)} %multiply_convert_fusion), kind=kOutput, calls=%fused_computation.28 | convolution fusion | flops 1174732800 | bytes 16482304 | tf_op jit(solution)/shard_map/efd,esd->fes/dot_general | solution.py:65
  72.0 0.0 reduce-scatter.2.cloned.1.call-update
  72.0 8.7 %fusion.1 = bf16[4,80]{1,0:T(4,128)(2,1)S(1)} fusion(bf16[4,1024,1792]{2,1,0:T(8,128)(2,1)} %param.17, f32[4,80,1792]{2,0,1:T(4,128)} %bitcast.140, bf16[1024,4,80]{0,2,1:T(8,128)(2,1)S(1)} %copy-done.4, bf16[1024,4,80]{0,2,1:T(8,128)(2,1)S(1)} %copy-done.2), kind=kOutput, calls=%fused_computation.16 | convolution fusion | flops 1178173184 | bytes 18285184 | tf_op jit(solution)/shard_map/fes,efd->esd/dot_general | solution.py:62
  80.7 11.3 %all-gather.1 = bf16[4,4,80]{2,1,0:T(4,128)(2,1)S(1)} all-gather(bf16[1,4,80]{2,1,0:T(4,128)(2,1)S(1)} %bitcast.145), channel_id=2, replica_groups=mesh['ex'=4,'ey'=2,'tp'=4] {'tp'}, dimensions={0}, use_global_device_ids=true | all-gather | bytes 3200 | tf_op jit(solution)/shard_map/all_gather | solution.py:74
  92.0 0.7 copy.77
  92.8 4.0 %all-to-all-start.3 = ((bf16[4,80,1]{0,2,1:T(2,128)(2,1)}), bf16[4,80,1]{0,2,1:T(2,128)(2,1)S(1)}, u32[]{:S(2)}, u32[]{:S(2)}) async-start(bf16[4,80,1]{0,2,1:T(2,128)(2,1)} %copy.77), calls=%async_computation.4 | async-start | bytes 81920 | tf_op jit(solution)/shard_map/all_to_all | solution.py:95
  96.7 7.6 %convolution_convert_fusion = bf16[4,1024,1792]{2,1,0:T(8,128)(2,1)} fusion(bf16[4,80,1792]{2,0,1:T(4,128)(2,1)S(1)} %multiply_convert_fusion, bf16[1024,4,80]{0,2,1:T(8,128)(2,1)S(1)} %copy-done.4, bf16[1024,4,80]{0,2,1:T(8,128)(2,1)S(1)} %copy-done.2), kind=kOutput, calls=%fused_computation | convolution fusion | flops 1184366592 | bytes 17137664 | tf_op jit(solution)/shard_map/fes,esd->efd/dot_general | solution.py:89
  104.3 2.1 %copy.80 = bf16[8,4,10,1792]{3,1,2,0:T(4,128)(2,1)S(1)} copy(bf16[8,4,10,1792]{3,2,1,0:T(8,128)(2,1)} %bitcast.37) | data formatting | bytes 2293760 | tf_op jit(solution)/shard_map/all_to_all | solution.py:53
  106.4 0.1 copy.78
  106.5 0.1 all_to_all.55
  106.6 0.1 reshape.189
  106.8 0.2 fusion.28
  106.9 0.2 fusion.26
  107.1 0.2 fusion.24
  107.2 0.2 fusion.22
  107.4 0.2 fusion.20
  107.5 0.2 fusion.18
  107.7 0.2 fusion.16
  107.8 0.2 fusion.14
  108.0 0.6 concatenate.4
  108.6 17.0 %all_gather.6 = bf16[1024,4,80]{0,2,1:T(8,128)(2,1)S(1)} all-gather(bf16[256,4,80]{0,2,1:T(8,128)(2,1)} %reduce-scatter.2.cloned.1.call-done), channel_id=1, replica_groups=mesh['ex'=4,'ey'=2,'tp'=4] {'tp'}, dimensions={0}, use_global_device_ids=true | all-gather | bytes 819200 | tf_op jit(solution)/shard_map/all_gather | solution.py:73
  125.6 11.1 %fusion.84 = f32[4,80,1792]{2,1,0:T(8,128)} fusion(bf16[4,1792,1024]{2,1,0:T(8,128)(2,1)} %param.15, bf16[1024,4,80]{0,2,1:T(8,128)(2,1)S(1)} %copy-done.4, bf16[1024,4,80]{0,2,1:T(8,128)(2,1)S(1)} %all_gather.6, bf16[1024,4,80]{0,2,1:T(8,128)(2,1)S(1)} %copy-done.2), kind=kOutput, calls=%fused_computation.133 | convolution fusion | flops 1178664960 | bytes 18939904 | tf_op jit(solution)/shard_map/fes,edf->esd/dot_general | solution.py:78
  136.8 11.4 %fusion = bf16[4,80,1792]{2,1,0:T(8,128)(2,1)} fusion(f32[4,80,1792]{2,1,0:T(8,128)} %fusion.84, bf16[4,1792,1024]{2,1,0:T(8,128)(2,1)} %param.16, bf16[1024,4,80]{0,2,1:T(8,128)(2,1)S(1)} %copy-done.2, bf16[1024,4,80]{0,2,1:T(8,128)(2,1)S(1)} %all_gather.6), kind=kOutput, calls=%fused_computation.5 | convolution fusion | flops 1178173440 | bytes 19431424 | tf_op jit(solution)/shard_map/fes,edf->esd/dot_general | solution.py:79
  148.1 2.9 %copy.74 = bf16[4,80,1792]{2,0,1:T(4,128)(2,1)} copy(bf16[4,80,1792]{2,1,0:T(8,128)(2,1)} %fusion) | data formatting | bytes 2293760 | tf_op jit(solution)/shard_map/convert_element_type | solution.py:82
  151.0 4.5 %all-to-all-start.2 = ((bf16[4,80,1792]{2,0,1:T(4,128)(2,1)}), bf16[4,80,1792]{2,0,1:T(4,128)(2,1)}, u32[]{:S(2)}, u32[]{:S(2)}) async-start(bf16[4,80,1792]{2,0,1:T(4,128)(2,1)} %copy.74), calls=%async_computation.3 | async-start | bytes 2293760 | tf_op jit(solution)/shard_map/all_to_all | solution.py:94
  155.5 7.6 %convolution_convert_fusion.2 = bf16[4,1792,1024]{2,1,0:T(8,128)(2,1)} fusion(bf16[4,80,1792]{2,0,1:T(4,128)(2,1)S(1)} %bitcast.138, bf16[1024,4,80]{0,2,1:T(8,128)(2,1)S(1)} %copy-done.4, bf16[1024,4,80]{0,2,1:T(8,128)(2,1)S(1)} %all_gather.6, bf16[1024,4,80]{0,2,1:T(8,128)(2,1)S(1)} %copy-done.2), kind=kOutput, calls=%fused_computation.2 | convolution fusion | flops 1186004992 | bytes 17793024 | tf_op jit(solution)/shard_map/esd,fes->edf/dot_general | solution.py:83
  163.1 7.6 %convolution_convert_fusion.1 = bf16[4,1792,1024]{2,1,0:T(8,128)(2,1)} fusion(bf16[4,80,1792]{2,0,1:T(4,128)(2,1)S(1)} %bitcast.139, bf16[1024,4,80]{0,2,1:T(8,128)(2,1)S(1)} %copy-done.2, bf16[1024,4,80]{0,2,1:T(8,128)(2,1)S(1)} %all_gather.6), kind=kOutput, calls=%fused_computation.1 | convolution fusion | flops 1184366592 | bytes 17137664 | tf_op jit(solution)/shard_map/esd,fes->edf/dot_general | solution.py:86
  170.7 1.0 all-to-all-done.2
  171.7 1.5 copy.75
  173.2 0.4 reshape.162
  173.7 1.1 convolution_convert_fusion.5
  (23 shorter events, 0.2 us)
Async XLA Ops:
  7.2 15.1 %copy-start = (bf16[32,1792]{1,0:T(8,128)(2,1)S(1)}, bf16[32,1792]{1,0:T(8,128)(2,1)}, u32[]{:S(2)}) copy-start(bf16[32,1792]{1,0:T(8,128)(2,1)} %param.10) | copy-start | bytes 344068
  17.1 10.0 %all-to-all-start = ((bf16[32,10,1]{1,2,0:T(2,128)(2,1)}), bf16[32,10,1]{1,2,0:T(2,128)(2,1)S(1)}, u32[]{:S(2)}, u32[]{:S(2)}) async-start(bf16[32,10,1]{1,2,0:T(2,128)(2,1)} %reshape.205), calls=%async_computation | async-start | bytes 32768 | tf_op jit(solution)/shard_map/all_to_all | solution.py:55
  24.2 6.4 %copy-start.5 = (bf16[32,1792]{1,0:T(8,128)(2,1)S(1)}, bf16[32,1792]{1,0:T(8,128)(2,1)}, u32[]{:S(2)}) copy-start(bf16[32,1792]{1,0:T(8,128)(2,1)} %param.9) | copy-start | bytes 344068
  27.0 27.3 %all-to-all-start.1 = ((bf16[32,10,1792]{2,1,0:T(8,128)(2,1)}), bf16[32,10,1792]{2,1,0:T(8,128)(2,1)S(1)}, u32[]{:S(2)}, u32[]{:S(2)}) async-start(bf16[32,10,1792]{2,1,0:T(8,128)(2,1)} %reshape.161), calls=%async_computation.1 | async-start | bytes 3670016 | tf_op jit(solution)/shard_map/all_to_all | solution.py:54
  54.4 38.4 %all-to-all-start.4 = ((bf16[32,10,1792]{2,1,0:T(8,128)(2,1)}), bf16[32,10,1792]{2,1,0:T(8,128)(2,1)}, u32[]{:S(2)}, u32[]{:S(2)}) async-start(bf16[32,10,1792]{2,1,0:T(8,128)(2,1)} %reshape.164), calls=%async_computation.5 | async-start | bytes 3670016 | tf_op jit(solution)/shard_map/all_to_all | solution.py:53
  58.7 49.9 %reduce-scatter.2.cloned.1.call-start = ((), (), s32[]{:S(2)}) async-start(), calls=%async_computation.6 | async-start | bytes 819200 | tf_op jit(solution)/shard_map/reduce_scatter | solution.py:64
  59.3 1.4 copy-start.3
  61.3 10.7 %copy-start.2 = (bf16[1024,4,80]{0,2,1:T(8,128)(2,1)S(1)}, bf16[1024,4,80]{0,2,1:T(8,128)(2,1)}, u32[]{:S(2)}) copy-start(bf16[1024,4,80]{0,2,1:T(8,128)(2,1)} %param.13) | copy-start | bytes 1966084
  61.3 10.7 %copy-start.4 = (bf16[1024,4,80]{0,2,1:T(8,128)(2,1)S(1)}, bf16[1024,4,80]{0,2,1:T(8,128)(2,1)}, u32[]{:S(2)}) copy-start(bf16[1024,4,80]{0,2,1:T(8,128)(2,1)} %param.14) | copy-start | bytes 1966084
  92.8 13.7 %all-to-all-start.3 = ((bf16[4,80,1]{0,2,1:T(2,128)(2,1)}), bf16[4,80,1]{0,2,1:T(2,128)(2,1)S(1)}, u32[]{:S(2)}, u32[]{:S(2)}) async-start(bf16[4,80,1]{0,2,1:T(2,128)(2,1)} %copy.77), calls=%async_computation.4 | async-start | bytes 81920 | tf_op jit(solution)/shard_map/all_to_all | solution.py:95
  151.0 20.7 %all-to-all-start.2 = ((bf16[4,80,1792]{2,0,1:T(4,128)(2,1)}), bf16[4,80,1792]{2,0,1:T(4,128)(2,1)}, u32[]{:S(2)}, u32[]{:S(2)}) async-start(bf16[4,80,1792]{2,0,1:T(4,128)(2,1)} %copy.74), calls=%async_computation.3 | async-start | bytes 2293760 | tf_op jit(solution)/shard_map/all_to_all | solution.py:94
  173.2 1.5 copy-start.1
Sparse Core Ops, SparseCore 0:
  72.1 24.1 reduce-scatter.1
where the time goes:
time: 182 us
  matrix products  74.8 us (41%)
  blocking collectives  28.3 us (16%)
  waiting for transfers between devices  25.4 us (14%)
  starting transfers between devices  21.6 us (12%)
  local copies, waits for them, and re-layouts  15.9 us (9%)
  between operations  14.3 us (8%)
    all_to_all x1, waiting for transfers between devices, on_device(): lax.all_to_all(send_dy, ('ex', 'ey'), split_axis=0, concat_axis=1, tiled=...  21.6 us
    all_gather x1, blocking collectives, on_device(): lax.all_gather(dh_local, 'tp', axis=0, tiled=True)  17 us
    dot_general x1, matrix products, on_device(): jnp.einsum('fes,edf->esd', d_up_pre, w_up, preferred_element_type=jnp.flo...  11.4 us
    all_gather x1, blocking collectives, on_device(): lax.all_gather(score_part[None], 'tp', axis=0, tiled=True)  11.3 us
    dot_general x1, matrix products, on_device(): jnp.einsum('fes,edf->esd', d_gate_pre, w_gate, preferred_element_type=jnp...  11.1 us
    dot_general x1, matrix products, on_device(): jnp.einsum('efd,esd->fes', w_down, scaled, preferred_element_type=jnp.flo...  10.6 us
    dot_general x1, matrix products, on_device(): jnp.einsum('fes,efd->esd', hidden, w_down, preferred_element_type=jnp.flo...  8.72 us
    dot_general x1, matrix products, on_device(): jnp.einsum('esd,fes->edf', recv_x, d_gate_pre, preferred_element_type=jnp...  7.62 us
  transfers between devices with their start and end apart: 6, of which 3 were waited for; matrix products, arithmetic and copies ran while one was open for 29% of the time, Pallas kernels for 0%

commit v1 on v0

--- a/solution.py
+++ b/solution.py
@@ -51,7 +51,15 @@
     send_gate = send_gate.astype(jnp.bfloat16).reshape(expert_count, capacity, 1)
     recv_x, recv_dy, recv_gate = (
         lax.all_to_all(send_x, ("ex", "ey"), split_axis=0, concat_axis=1, tiled=True),
-        lax.all_to_all(send_dy, ("ex", "ey"), split_axis=0, concat_axis=1, tiled=True),
+        jnp.concatenate(
+            lax.all_to_all(
+                jnp.stack(jnp.split(send_dy, lax.axis_size(("ex", "ey")), axis=0)),
+                ("ex", "ey"),
+                0,
+                0,
+            ),
+            axis=1,
+        ),
         lax.all_to_all(send_gate, ("ex", "ey"), split_axis=0, concat_axis=1, tiled=True),
     )
     scaled = (recv_gate.astype(jnp.float32) * recv_dy.astype(jnp.float32)).astype(jnp.bfloat16)

time: 182 us -> 175 us (0.962)
  waiting for transfers between devices: 25.4 us -> 14.5 us
  local copies, waits for them, and re-layouts: 15.9 us -> 19 us
    all_to_all x1, waiting for transfers between devices: 21.6 us -> 13.5 us  [on_device(): lax.all_to_all(jnp.stack(jnp.split(send_dy, lax.axis_size(('ex', 'ey')),...]
    another operation x2 -> x12, local copies, waits for them, and re-layouts: 0.12 us -> 3.07 us  [the longest x10 2.94 us: on_device(): jnp.stack(jnp.split(send_dy, lax.axis_size(('ex', 'ey')), axis=0))]
    all_to_all x1, waiting for transfers between devices: 2.8 us -> 0.01 us  [on_device(): lax.all_to_all(send_gate, ('ex', 'ey'), split_axis=0, concat_axis=1, tile...]
  transfers between devices with their start and end apart: 6 -> 6, of which waited for: 3 -> 2; matrix products, arithmetic and copies ran while one was open for 29% -> 31% of each run, Pallas kernels for 0% -> 0%
where the time goes in v1:
time: 175 us; the launch traced here: 174 us
  matrix products  74.1 us (42%)
  blocking collectives  28.4 us (16%)
  starting transfers between devices  22.4 us (13%)
  local copies, waits for them, and re-layouts  19 us (11%)
  between operations  14.6 us (8%)
  waiting for transfers between devices  14.5 us (8%)
    all_gather x1, blocking collectives, on_device(): lax.all_gather(dh_local, 'tp', axis=0, tiled=True)  17.1 us
    all_to_all x1, waiting for transfers between devices, on_device(): lax.all_to_all(jnp.stack(jnp.split(send_dy, lax.axis_size(('ex', 'ey')),...  13.5 us
    dot_general x1, matrix products, on_device(): jnp.einsum('fes,edf->esd', d_up_pre, w_up, preferred_element_type=jnp.flo...  11.4 us
    all_gather x1, blocking collectives, on_device(): lax.all_gather(score_part[None], 'tp', axis=0, tiled=True)  11.3 us
    dot_general x1, matrix products, on_device(): jnp.einsum('fes,edf->esd', d_gate_pre, w_gate, preferred_element_type=jnp...  11.1 us
    dot_general x1, matrix products, on_device(): jnp.einsum('efd,esd->fes', w_down, scaled, preferred_element_type=jnp.flo...  10.5 us
    dot_general x1, matrix products, on_device(): jnp.einsum('fes,efd->esd', hidden, w_down, preferred_element_type=jnp.flo...  8.15 us
    dot_general x1, matrix products, on_device(): jnp.einsum('fes,esd->efd', hidden, scaled, preferred_element_type=jnp.flo...  7.62 us
  transfers between devices with their start and end apart: 6, of which 2 were waited for; matrix products, arithmetic and copies ran while one was open for 31% of the time, Pallas kernels for 0%

profile of v1, /device:TPU:0, one launch (start us, length us, event | category | flops | bytes accessed | tf_op | source)
XLA Modules:
  0.0 174.4 jit_solution(9004810564996971288)
XLA Ops:
  7.2 0.8 copy.64
  8.0 0.1 eq.145
  8.1 0.1 eq.149
  8.2 0.6 reduce-window.6
  8.8 0.2 slice_reduce_fusion
  9.0 0.1 fusion.66
  9.2 0.3 slice_reduce_fusion.7
  9.6 0.9 convolution_reduce_fusion
  10.5 0.9 convolution_reduce_fusion.1
  11.3 0.9 convolution_reduce_fusion.2
  12.2 0.9 convolution_reduce_fusion.3
  13.0 0.9 convolution_reduce_fusion.4
  13.9 0.9 convolution_reduce_fusion.5
  14.7 0.9 convolution_reduce_fusion.7
  15.6 0.9 convolution_reduce_fusion.6
  16.4 0.7 reshape.217
  17.2 5.2 %all-to-all-start = ((bf16[32,10,1]{1,2,0:T(2,128)(2,1)}), bf16[32,10,1]{1,2,0:T(2,128)(2,1)}, u32[]{:S(2)}, u32[]{:S(2)}) async-start(bf16[32,10,1]{1,2,0:T(2,128)(2,1)} %reshape.217), calls=%async_computation | async-start | bytes 32768 | tf_op jit(solution)/shard_map/all_to_all | solution.py:63
  22.4 0.5 convolution_convert_fusion.4
  23.0 0.8 fusion.86
  24.1 0.7 copy-done.6
  24.9 1.0 stack.34
  26.0 1.6 copy.72
  27.7 4.3 %all-to-all-start.1 = ((bf16[8,4,10,1792]{3,1,2,0:T(4,128)(2,1)}), bf16[8,4,10,1792]{3,1,2,0:T(4,128)(2,1)S(1)}, u32[]{:S(2)}, u32[]{:S(2)}) async-start(bf16[8,4,10,1792]{3,1,2,0:T(4,128)(2,1)} %copy.72), calls=%async_computation.1 | async-start | bytes 2293760 | tf_op jit(solution)/shard_map/all_to_all | solution.py:55
  32.1 0.5 convolution_convert_fusion.3
  32.6 1.4 reshape.177
  34.0 0.7 copy.69
  34.8 0.1 reshape.178
  34.9 0.1 copy.71
  35.0 13.5 %all-to-all-done.1 = bf16[8,4,10,1792]{3,1,2,0:T(4,128)(2,1)S(1)} async-done(((bf16[8,4,10,1792]{3,1,2,0:T(4,128)(2,1)}), bf16[8,4,10,1792]{3,1,2,0:T(4,128)(2,1)S(1)}, u32[]{:S(2)}, u32[]{:S(2)}) %all-to-all-start.1) | async-done | bytes 1146912 | tf_op jit(solution)/shard_map/all_to_all | solution.py:55
  48.4 4.3 %all-to-all-start.4 = ((bf16[32,10,1792]{2,1,0:T(8,128)(2,1)}), bf16[32,10,1792]{2,1,0:T(8,128)(2,1)}, u32[]{:S(2)}, u32[]{:S(2)}) async-start(bf16[32,10,1792]{2,1,0:T(8,128)(2,1)} %reshape.177), calls=%async_computation.5 | async-start | bytes 3670016 | tf_op jit(solution)/shard_map/all_to_all | solution.py:53
  52.8 0.5 multiply_convert_fusion
  53.3 10.5 %fusion.12 = bf16[1024,4,80]{0,2,1:T(8,128)(2,1)} fusion(bf16[4,1024,1792]{2,1,0:T(8,128)(2,1)} %param.17, bf16[4,80,1792]{2,0,1:T(4,128)(2,1)S(1)} %multiply_convert_fusion), kind=kOutput, calls=%fused_computation.28 | convolution fusion | flops 1174732800 | bytes 16482304 | tf_op jit(solution)/shard_map/efd,esd->fes/dot_general | solution.py:73
  63.9 0.2 convert_element_type.167
  64.1 0.9 copy-done.2
  65.0 0.2 copy-done.3
  65.2 8.2 %fusion.1 = bf16[4,80]{1,0:T(4,128)(2,1)S(1)} fusion(bf16[4,1024,1792]{2,1,0:T(8,128)(2,1)} %param.17, f32[4,80,1792]{2,0,1:T(4,128)S(1)} %bitcast.138, bf16[1024,4,80]{0,2,1:T(8,128)(2,1)S(1)} %copy-done.3, bf16[1024,4,80]{0,2,1:T(8,128)(2,1)S(1)} %copy-done.2), kind=kOutput, calls=%fused_computation.16 | convolution fusion | flops 1178173184 | bytes 18285184 | tf_op jit(solution)/shard_map/fes,efd->esd/dot_general | solution.py:70
  73.3 11.3 %all-gather.1 = bf16[4,4,80]{2,1,0:T(4,128)(2,1)S(1)} all-gather(bf16[1,4,80]{2,1,0:T(4,128)(2,1)S(1)} %bitcast.142), channel_id=2, replica_groups=mesh['ex'=4,'ey'=2,'tp'=4] {'tp'}, dimensions={0}, use_global_device_ids=true | all-gather | bytes 3200 | tf_op jit(solution)/shard_map/all_gather | solution.py:82
  84.7 0.7 copy.77
  85.4 4.0 %all-to-all-start.3 = ((bf16[4,80,1]{0,2,1:T(2,128)(2,1)}), bf16[4,80,1]{0,2,1:T(2,128)(2,1)S(1)}, u32[]{:S(2)}, u32[]{:S(2)}) async-start(bf16[4,80,1]{0,2,1:T(2,128)(2,1)} %copy.77), calls=%async_computation.4 | async-start | bytes 81920 | tf_op jit(solution)/shard_map/all_to_all | solution.py:103
  89.5 7.6 %convolution_convert_fusion = bf16[4,1024,1792]{2,1,0:T(8,128)(2,1)} fusion(bf16[4,80,1792]{2,0,1:T(4,128)(2,1)S(1)} %multiply_convert_fusion, bf16[1024,4,80]{0,2,1:T(8,128)(2,1)S(1)} %copy-done.4, bf16[1024,4,80]{0,2,1:T(8,128)(2,1)S(1)} %copy-done.2), kind=kOutput, calls=%fused_computation | convolution fusion | flops 1184366592 | bytes 17137664 | tf_op jit(solution)/shard_map/fes,esd->efd/dot_general | solution.py:97
  97.1 2.2 %copy.80 = bf16[8,4,10,1792]{3,1,2,0:T(4,128)(2,1)S(1)} copy(bf16[8,4,10,1792]{3,2,1,0:T(8,128)(2,1)} %bitcast.36) | data formatting | bytes 2293760 | tf_op jit(solution)/shard_map/all_to_all | solution.py:53
  99.3 0.1 copy.78
  99.3 0.1 all_to_all.51
  99.5 0.1 reshape.201
  99.6 0.2 fusion.28
  99.7 0.2 fusion.26
  99.9 0.2 fusion.24
  100.0 0.2 fusion.22
  100.2 0.2 fusion.20
  100.3 0.2 fusion.18
  100.5 0.2 fusion.16
  100.6 0.2 fusion.14
  100.8 0.6 concatenate.4
  101.4 17.1 %all_gather.6 = bf16[1024,4,80]{0,2,1:T(8,128)(2,1)S(1)} all-gather(bf16[256,4,80]{0,2,1:T(8,128)(2,1)} %reduce-scatter.2.cloned.1.call-done), channel_id=1, replica_groups=mesh['ex'=4,'ey'=2,'tp'=4] {'tp'}, dimensions={0}, use_global_device_ids=true | all-gather | bytes 819200 | tf_op jit(solution)/shard_map/all_gather | solution.py:81
  118.5 11.1 %fusion.84 = f32[4,80,1792]{2,1,0:T(8,128)} fusion(bf16[4,1792,1024]{2,1,0:T(8,128)(2,1)} %param.15, bf16[1024,4,80]{0,2,1:T(8,128)(2,1)S(1)} %copy-done.5, bf16[1024,4,80]{0,2,1:T(8,128)(2,1)S(1)} %all_gather.6, bf16[1024,4,80]{0,2,1:T(8,128)(2,1)S(1)} %copy-done.2), kind=kOutput, calls=%fused_computation.141 | convolution fusion | flops 1178664960 | bytes 18939904 | tf_op jit(solution)/shard_map/fes,edf->esd/dot_general | solution.py:86
  129.6 11.4 %fusion = bf16[4,80,1792]{2,1,0:T(8,128)(2,1)} fusion(f32[4,80,1792]{2,1,0:T(8,128)} %fusion.84, bf16[4,1792,1024]{2,1,0:T(8,128)(2,1)} %param.16, bf16[1024,4,80]{0,2,1:T(8,128)(2,1)S(1)} %copy-done.2, bf16[1024,4,80]{0,2,1:T(8,128)(2,1)S(1)} %all_gather.6), kind=kOutput, calls=%fused_computation.5 | convolution fusion | flops 1178173440 | bytes 19431424 | tf_op jit(solution)/shard_map/fes,edf->esd/dot_general | solution.py:87
  141.0 2.9 %copy.74 = bf16[4,80,1792]{2,0,1:T(4,128)(2,1)} copy(bf16[4,80,1792]{2,1,0:T(8,128)(2,1)} %fusion) | data formatting | bytes 2293760 | tf_op jit(solution)/shard_map/convert_element_type | solution.py:90
  143.9 4.5 %all-to-all-start.2 = ((bf16[4,80,1792]{2,0,1:T(4,128)(2,1)}), bf16[4,80,1792]{2,0,1:T(4,128)(2,1)}, u32[]{:S(2)}, u32[]{:S(2)}) async-start(bf16[4,80,1792]{2,0,1:T(4,128)(2,1)} %copy.74), calls=%async_computation.3 | async-start | bytes 2293760 | tf_op jit(solution)/shard_map/all_to_all | solution.py:102
  148.3 7.6 %convolution_convert_fusion.2 = bf16[4,1792,1024]{2,1,0:T(8,128)(2,1)} fusion(bf16[4,80,1792]{2,0,1:T(4,128)(2,1)S(1)} %bitcast.136, bf16[1024,4,80]{0,2,1:T(8,128)(2,1)S(1)} %copy-done.5, bf16[1024,4,80]{0,2,1:T(8,128)(2,1)S(1)} %all_gather.6, bf16[1024,4,80]{0,2,1:T(8,128)(2,1)S(1)} %copy-done.2), kind=kOutput, calls=%fused_computation.2 | convolution fusion | flops 1186004992 | bytes 17793024 | tf_op jit(solution)/shard_map/esd,fes->edf/dot_general | solution.py:91
  156.0 7.6 %convolution_convert_fusion.1 = bf16[4,1792,1024]{2,1,0:T(8,128)(2,1)} fusion(bf16[4,80,1792]{2,0,1:T(4,128)(2,1)S(1)} %bitcast.137, bf16[1024,4,80]{0,2,1:T(8,128)(2,1)S(1)} %copy-done.2, bf16[1024,4,80]{0,2,1:T(8,128)(2,1)S(1)} %all_gather.6), kind=kOutput, calls=%fused_computation.1 | convolution fusion | flops 1184366592 | bytes 17137664 | tf_op jit(solution)/shard_map/esd,fes->edf/dot_general | solution.py:94
  163.5 1.0 all-to-all-done.2
  164.6 1.5 copy.75
  166.1 0.4 reshape.175
  166.5 1.1 convolution_convert_fusion.5
  (76 shorter events, 0.9 us)
Async XLA Ops:
  7.2 15.3 %copy-start = (bf16[32,1792]{1,0:T(8,128)(2,1)S(1)}, bf16[32,1792]{1,0:T(8,128)(2,1)}, u32[]{:S(2)}) copy-start(bf16[32,1792]{1,0:T(8,128)(2,1)} %param.10) | copy-start | bytes 344068
  9.5 12.9 %copy-start.8 = (s32[32]{0:T(128)}, s32[32]{0:T(128)S(1)}, u32[]{:S(2)}) copy-start(s32[32]{0:T(128)S(1)} %get-tuple-element.5) | copy-start | bytes 388
  9.5 12.8 %copy-start.10 = (s32[32]{0:T(128)}, s32[32]{0:T(128)S(1)}, u32[]{:S(2)}) copy-start(s32[32]{0:T(128)S(1)} %get-tuple-element.6) | copy-start | bytes 388
  9.5 12.8 %copy-start.12 = (s32[32]{0:T(128)}, s32[32]{0:T(128)S(1)}, u32[]{:S(2)}) copy-start(s32[32]{0:T(128)S(1)} %get-tuple-element.7) | copy-start | bytes 388
  9.5 12.8 %copy-start.14 = (s32[32]{0:T(128)}, s32[32]{0:T(128)S(1)}, u32[]{:S(2)}) copy-start(s32[32]{0:T(128)S(1)} %get-tuple-element.8) | copy-start | bytes 388
  9.6 12.8 %copy-start.16 = (s32[32]{0:T(128)}, s32[32]{0:T(128)S(1)}, u32[]{:S(2)}) copy-start(s32[32]{0:T(128)S(1)} %get-tuple-element.9) | copy-start | bytes 388
  9.6 12.8 %copy-start.18 = (s32[32]{0:T(128)}, s32[32]{0:T(128)S(1)}, u32[]{:S(2)}) copy-start(s32[32]{0:T(128)S(1)} %get-tuple-element.10) | copy-start | bytes 388
  9.6 12.8 %copy-start.20 = (s32[32]{0:T(128)}, s32[32]{0:T(128)S(1)}, u32[]{:S(2)}) copy-start(s32[32]{0:T(128)S(1)} %get-tuple-element.11) | copy-start | bytes 388
  9.6 12.8 %copy-start.22 = (s32[32]{0:T(128)}, s32[32]{0:T(128)S(1)}, u32[]{:S(2)}) copy-start(s32[32]{0:T(128)S(1)} %get-tuple-element.12) | copy-start | bytes 388
  17.2 10.5 %all-to-all-start = ((bf16[32,10,1]{1,2,0:T(2,128)(2,1)}), bf16[32,10,1]{1,2,0:T(2,128)(2,1)}, u32[]{:S(2)}, u32[]{:S(2)}) async-start(bf16[32,10,1]{1,2,0:T(2,128)(2,1)} %reshape.217), calls=%async_computation | async-start | bytes 32768 | tf_op jit(solution)/shard_map/all_to_all | solution.py:63
  23.8 0.9 copy-start.6
  27.6 4.4 %copy-start.7 = (bf16[32,1792]{1,0:T(8,128)(2,1)S(1)}, bf16[32,1792]{1,0:T(8,128)(2,1)}, u32[]{:S(2)}) copy-start(bf16[32,1792]{1,0:T(8,128)(2,1)} %param.9) | copy-start | bytes 344068
  27.6 4.4 %copy-start.9 = (s32[32]{0:T(128)S(1)}, s32[32]{0:T(128)}, u32[]{:S(2)}) copy-start(s32[32]{0:T(128)} %copy-done.8) | copy-start | bytes 388
  27.6 4.4 %copy-start.11 = (s32[32]{0:T(128)S(1)}, s32[32]{0:T(128)}, u32[]{:S(2)}) copy-start(s32[32]{0:T(128)} %copy-done.10) | copy-start | bytes 388
  27.6 4.4 %copy-start.13 = (s32[32]{0:T(128)S(1)}, s32[32]{0:T(128)}, u32[]{:S(2)}) copy-start(s32[32]{0:T(128)} %copy-done.12) | copy-start | bytes 388
  27.6 4.4 %copy-start.15 = (s32[32]{0:T(128)S(1)}, s32[32]{0:T(128)}, u32[]{:S(2)}) copy-start(s32[32]{0:T(128)} %copy-done.14) | copy-start | bytes 388
  27.6 4.4 %copy-start.17 = (s32[32]{0:T(128)S(1)}, s32[32]{0:T(128)}, u32[]{:S(2)}) copy-start(s32[32]{0:T(128)} %copy-done.16) | copy-start | bytes 388
  27.6 4.4 %copy-start.19 = (s32[32]{0:T(128)S(1)}, s32[32]{0:T(128)}, u32[]{:S(2)}) copy-start(s32[32]{0:T(128)} %copy-done.18) | copy-start | bytes 388
  27.6 4.4 %copy-start.21 = (s32[32]{0:T(128)S(1)}, s32[32]{0:T(128)}, u32[]{:S(2)}) copy-start(s32[32]{0:T(128)} %copy-done.20) | copy-start | bytes 388
  27.7 4.4 %copy-start.23 = (s32[32]{0:T(128)S(1)}, s32[32]{0:T(128)}, u32[]{:S(2)}) copy-start(s32[32]{0:T(128)} %copy-done.22) | copy-start | bytes 388
  27.7 20.8 %all-to-all-start.1 = ((bf16[8,4,10,1792]{3,1,2,0:T(4,128)(2,1)}), bf16[8,4,10,1792]{3,1,2,0:T(4,128)(2,1)S(1)}, u32[]{:S(2)}, u32[]{:S(2)}) async-start(bf16[8,4,10,1792]{3,1,2,0:T(4,128)(2,1)} %copy.72), calls=%async_computation.1 | async-start | bytes 2293760 | tf_op jit(solution)/shard_map/all_to_all | solution.py:55
  48.4 37.0 %all-to-all-start.4 = ((bf16[32,10,1792]{2,1,0:T(8,128)(2,1)}), bf16[32,10,1792]{2,1,0:T(8,128)(2,1)}, u32[]{:S(2)}, u32[]{:S(2)}) async-start(bf16[32,10,1792]{2,1,0:T(8,128)(2,1)} %reshape.177), calls=%async_computation.5 | async-start | bytes 3670016 | tf_op jit(solution)/shard_map/all_to_all | solution.py:53
  52.8 48.6 %reduce-scatter.2.cloned.1.call-start = ((), (), s32[]{:S(2)}) async-start(), calls=%async_computation.6 | async-start | bytes 819200 | tf_op jit(solution)/shard_map/reduce_scatter | solution.py:72
  63.9 1.1 copy-start.2
  63.9 1.3 copy-start.3
  65.2 24.3 %copy-start.4 = (bf16[1024,4,80]{0,2,1:T(8,128)(2,1)S(1)}, bf16[1024,4,80]{0,2,1:T(8,128)(2,1)}, u32[]{:S(2)}) copy-start(bf16[1024,4,80]{0,2,1:T(8,128)(2,1)} %param.14) | copy-start | bytes 1966084
  85.4 13.8 %all-to-all-start.3 = ((bf16[4,80,1]{0,2,1:T(2,128)(2,1)}), bf16[4,80,1]{0,2,1:T(2,128)(2,1)S(1)}, u32[]{:S(2)}, u32[]{:S(2)}) async-start(bf16[4,80,1]{0,2,1:T(2,128)(2,1)} %copy.77), calls=%async_computation.4 | async-start | bytes 81920 | tf_op jit(solution)/shard_map/all_to_all | solution.py:103
  97.1 21.4 %copy-start.5 = (bf16[1024,4,80]{0,2,1:T(8,128)(2,1)S(1)}, bf16[1024,4,80]{0,2,1:T(8,128)(2,1)}, u32[]{:S(2)}) copy-start(bf16[1024,4,80]{0,2,1:T(8,128)(2,1)} %param.14) | copy-start | bytes 1966084
  143.9 20.7 %all-to-all-start.2 = ((bf16[4,80,1792]{2,0,1:T(4,128)(2,1)}), bf16[4,80,1792]{2,0,1:T(4,128)(2,1)}, u32[]{:S(2)}, u32[]{:S(2)}) async-start(bf16[4,80,1792]{2,0,1:T(4,128)(2,1)} %copy.74), calls=%async_computation.3 | async-start | bytes 2293760 | tf_op jit(solution)/shard_map/all_to_all | solution.py:102
  166.1 1.5 copy-start.1
Sparse Core Ops, SparseCore 0:
  64.0 24.3 reduce-scatter.1
